TPU v7x, 32 devices: a whole 2x2x4 slice. The times are simulated.
32 devices in a mesh: groups: 1, wide: 8 (over y, x, core), narrow: 4 (over z).
Axes of the slice: x: 2, y: 2, z: 4, core: 2. Of those that a mesh axis runs over, the one named last changes fastest.
Arguments:
- table_cells: bfloat16 [128, 128, 192], P(('groups', 'wide', 'narrow')), may hold values from -12 to 12
- counts: int32 [128], P(('groups', 'wide', 'narrow')), may hold values from 32 to 128, as said below
- train_count: int32 [1], P('groups'), may hold values from 32 to 96
- norm_gain: float32 [3, 192], replicated, may hold values from 0.5 to 1.5
- feature_in: bfloat16 [192, 576], P('narrow'), may hold values from -0.4375 to 0.4375
- feature_out: bfloat16 [192, 192], P('narrow'), may hold values from -0.4375 to 0.4375
- sample_in: bfloat16 [192, 576], P('narrow'), may hold values from -0.4375 to 0.4375
- sample_out: bfloat16 [192, 192], P('narrow'), may hold values from -0.4375 to 0.4375
- hidden_up: bfloat16 [192, 768], P('narrow'), may hold values from -0.4375 to 0.4375
- hidden_down: bfloat16 [768, 192], P('narrow'), may hold values from -0.21875 to 0.21875
Outputs:
- updated_cells: bfloat16 [128, 128, 192], P(('groups', 'wide', 'narrow'))
Inputs may be any that keep to these rules, and one draw needn't show every extreme that they name: `counts`: feature j of a row is present when j < its count; some row has all 128 features present. Rows 0 to train_count - 1 are the training rows.
All inputs are finite; a program needn't handle non-finite values.
Results may differ from a plain program's by a relative error of at most 0.0086.
Values may be sent and summed in bfloat16 or wider, within the bound.
A program may use at most 64 MiB of HBM per device.

v0:
```python
import jax
import jax.numpy as jnp
from jax import lax
from jax.sharding import PartitionSpec as P

HEADS = 6
epsilon = 1e-05


def normalize(values, gain):
    average = jnp.mean(values, axis=-1, keepdims=True)
    centered = values - average
    spread = jnp.mean(centered * centered, axis=-1, keepdims=True)
    return centered * lax.rsqrt(spread + epsilon) * gain


def attend(packed, valid, head_count):
    length = packed.shape[0]
    model_width = packed.shape[1] // 3
    head_size = model_width // head_count
    scale_factor = 1.0 / jnp.sqrt(jnp.float32(head_size))
    queries = packed[:, :model_width].reshape(length, head_count, head_size)
    key_part = packed[:, model_width : 2 * model_width].reshape(length, head_count, head_size)
    value_part = packed[:, 2 * model_width :].reshape(length, head_count, head_size)
    scores = (
        jnp.einsum("qhd,khd->hqk", queries, key_part, preferred_element_type=jnp.float32)
        * scale_factor
    )
    scores = jnp.where(valid[None, None, :], scores, jnp.float32(-1e30))
    maxima = jnp.max(scores, axis=-1, keepdims=True)
    exponentials = jnp.where(valid[None, None, :], jnp.exp(scores - maxima), jnp.float32(0.0))
    totals = jnp.sum(exponentials, axis=-1, keepdims=True)
    probabilities = (exponentials / totals).astype(jnp.bfloat16)
    context = jnp.einsum(
        "hqk,khd->qhd", probabilities, value_part, preferred_element_type=jnp.float32
    )
    return context.reshape(length, model_width).astype(jnp.bfloat16)


def project(values, weight):
    flat = values.reshape(-1, values.shape[-1])
    return jnp.dot(flat, weight, preferred_element_type=jnp.float32).reshape(
        values.shape[:-1] + (weight.shape[1],)
    )


def body(
    table_cells,
    counts,
    train_count,
    norm_gain,
    feature_in,
    feature_out,
    sample_in,
    sample_out,
    hidden_up,
    hidden_down,
):
    row_local, feats_all, model_width = table_cells.shape
    feat_in_all, feat_out_all = (
        lax.all_gather(feature_in, "narrow", axis=0, tiled=True),
        lax.all_gather(feature_out, "narrow", axis=0, tiled=True),
    )
    feature_ids = jnp.arange(feats_all, dtype=jnp.int32)
    packed = project(table_cells, feat_in_all).astype(jnp.bfloat16)

    def feature_row(pair):
        return attend(pair[0], feature_ids < pair[1], HEADS)

    context = lax.map(feature_row, (packed, counts))
    update = project(context, feat_out_all)
    first = normalize(table_cells.astype(jnp.float32) + update, norm_gain[0]).astype(jnp.bfloat16)
    columns = lax.all_to_all(first, ("wide", "narrow"), split_axis=1, concat_axis=0, tiled=True)
    rows_all, feat_local = (columns.shape[0], columns.shape[1])
    samp_in_all, samp_out_all = (
        lax.all_gather(sample_in, "narrow", axis=0, tiled=True),
        lax.all_gather(sample_out, "narrow", axis=0, tiled=True),
    )
    by_feature = jnp.swapaxes(columns, 0, 1)
    valid = jnp.arange(rows_all, dtype=jnp.int32) < train_count[0]
    packed_samples = project(by_feature, samp_in_all).astype(jnp.bfloat16)
    sample_context = lax.map(lambda column: attend(column, valid, HEADS), packed_samples)
    sample_update = project(sample_context, samp_out_all)
    second = normalize(by_feature.astype(jnp.float32) + sample_update, norm_gain[1]).astype(
        jnp.bfloat16
    )
    up_all, down_all = (
        lax.all_gather(hidden_up, "narrow", axis=0, tiled=True),
        lax.all_gather(hidden_down, "narrow", axis=0, tiled=True),
    )
    hidden = jax.nn.gelu(project(second, up_all), approximate=False).astype(jnp.bfloat16)
    back = project(hidden, down_all)
    result = normalize(second.astype(jnp.float32) + back, norm_gain[2]).astype(jnp.bfloat16)
    result_rows = jnp.swapaxes(result, 0, 1)
    return lax.all_to_all(result_rows, ("wide", "narrow"), split_axis=0, concat_axis=1, tiled=True)


def solution(mesh):
    return jax.shard_map(
        body,
        mesh=mesh,
        in_specs=(
            P(("groups", "wide", "narrow"), None, None),
            P(("groups", "wide", "narrow")),
            P("groups"),
            P(),
            P("narrow", None),
            P("narrow", None),
            P("narrow", None),
            P("narrow", None),
            P("narrow", None),
            P("narrow", None),
        ),
        out_specs=P(("groups", "wide", "narrow"), None, None),
        check_vma=False,
    )
```

profile of v0, /device:TPU:0, one launch (start us, length us, event | category | flops | bytes accessed | tf_op | source)
XLA Modules:
  0.0 134.4 jit_solution(16577640377260590868)
XLA Ops:
  0.0 0.8 fusion.94
  0.8 15.2 %all_gather.19 = bf16[192,192]{1,0:T(8,128)(2,1)S(1)} all-gather(bf16[48,192]{1,0:T(8,128)(2,1)} %param.19), channel_id=1, replica_groups=mesh['groups'=1,'wide'=8,'narrow'=4] {'narrow'}, dimensions={0}, use_global_device_ids=true | all-gather | bytes 92160 | tf_op jit(solution)/shard_map/all_gather | solution.py:62
  16.0 14.4 %all_gather.18 = bf16[192,576]{1,0:T(8,128)(2,1)S(1)} all-gather(bf16[48,576]{1,0:T(8,128)(2,1)} %param.18), channel_id=1, replica_groups=mesh['groups'=1,'wide'=8,'narrow'=4] {'narrow'}, dimensions={0}, use_global_device_ids=true | all-gather | bytes 276480 | tf_op jit(solution)/shard_map/all_gather | solution.py:61
  30.5 1.3 convolution_convert_fusion.3
  31.8 9.3 %while.22 = (s32[]{:T(128)}, bf16[4,128,192]{1,2,0:T(8,128)(2,1)S(1)}, bf16[4,128,576]{1,2,0:T(8,128)(2,1)S(1)}, s32[4]{0:T(128)S(1)}, s32[]{:T(128)}) while((s32[]{:T(128)}, bf16[4,128,192]{1,2,0:T(8,128)(2,1)S(1)}, bf16[4,128,576]{1,2,0:T(8,128)(2,1)S(1)}, s32[4]{0:T(128)S(1)}, s32[]{:T(128)}) %tuple.61), condition=%wide.region_3.4_spmd.clone, body=%wide.region_0.3_spmd.clone.sunk | while | flops 19981440 | bytes 1776221 | solution.py:70
  31.8 0.7 dynamic_slice.20
  32.5 0.7 iota_compare_fusion.4
  33.2 0.4 fusion.137
  33.6 0.3 fusion.138
  34.1 0.7 dynamic_slice.20
  34.8 0.7 iota_compare_fusion.4
  35.6 0.4 fusion.137
  35.9 0.3 fusion.138
  36.5 0.7 dynamic_slice.20
  37.1 0.7 iota_compare_fusion.4
  37.9 0.4 fusion.137
  38.2 0.3 fusion.138
  38.8 0.7 dynamic_slice.20
  39.5 0.7 iota_compare_fusion.4
  40.2 0.4 fusion.137
  40.6 0.3 fusion.138
  41.1 0.3 fusion.95
  41.6 0.9 copy.28
  42.5 5.3 %all-to-all-start = ((bf16[4,128,192]{2,0,1:T(4,128)(2,1)}), bf16[4,128,192]{2,0,1:T(4,128)(2,1)S(1)}, u32[]{:S(2)}, u32[]{:S(2)}) async-start(bf16[4,128,192]{2,0,1:T(4,128)(2,1)} %copy.28), calls=%async_computation | async-start | bytes 524288 | tf_op jit(solution)/shard_map/all_to_all | solution.py:73
  47.8 16.4 %all_gather.21 = bf16[192,192]{1,0:T(8,128)(2,1)S(1)} all-gather(bf16[48,192]{1,0:T(8,128)(2,1)S(1)} %copy-done.4), channel_id=1, replica_groups=mesh['groups'=1,'wide'=8,'narrow'=4] {'narrow'}, dimensions={0}, use_global_device_ids=true | all-gather | bytes 92160 | tf_op jit(solution)/shard_map/all_gather | solution.py:77
  64.3 13.8 %all_gather.20 = bf16[192,576]{1,0:T(8,128)(2,1)S(1)} all-gather(bf16[48,576]{1,0:T(8,128)(2,1)S(1)} %copy-done.3), channel_id=1, replica_groups=mesh['groups'=1,'wide'=8,'narrow'=4] {'narrow'}, dimensions={0}, use_global_device_ids=true | all-gather | bytes 276480 | tf_op jit(solution)/shard_map/all_gather | solution.py:76
  78.1 14.3 %all_gather.22 = bf16[192,768]{1,0:T(8,128)(2,1)S(1)} all-gather(bf16[48,768]{1,0:T(8,128)(2,1)S(1)} %copy-done.2), channel_id=1, replica_groups=mesh['groups'=1,'wide'=8,'narrow'=4] {'narrow'}, dimensions={0}, use_global_device_ids=true | all-gather | bytes 368640 | tf_op jit(solution)/shard_map/all_gather | solution.py:88
  92.3 14.2 %all_gather.23 = bf16[768,192]{1,0:T(8,128)(2,1)S(1)} all-gather(bf16[192,192]{1,0:T(8,128)(2,1)S(1)} %copy-done.1), channel_id=1, replica_groups=mesh['groups'=1,'wide'=8,'narrow'=4] {'narrow'}, dimensions={0}, use_global_device_ids=true | all-gather | bytes 368640 | tf_op jit(solution)/shard_map/all_gather | solution.py:89
  106.9 0.4 convolution_convert_fusion.2
  107.3 6.4 %while.23 = (s32[]{:T(128)}, bf16[4,128,192]{1,2,0:T(8,128)(2,1)S(1)}, bf16[4,128,576]{1,2,0:T(8,128)(2,1)S(1)}, s32[]{:T(128)}, s32[]{:T(128)}) while((s32[]{:T(128)}, bf16[4,128,192]{1,2,0:T(8,128)(2,1)S(1)}, bf16[4,128,576]{1,2,0:T(8,128)(2,1)S(1)}, s32[]{:T(128)}, s32[]{:T(128)}) %tuple.58), condition=%wide.region_9.10_spmd.clone, body=%wide.region_6.9_spmd.clone.sunk | while | flops 19981440 | bytes 1776209 | solution.py:82
  107.3 0.7 iota_compare_fusion.5
  108.0 0.4 fusion.146
  108.4 0.3 fusion.147
  108.6 0.2 convolution_convert_fusion.7
  108.9 0.7 iota_compare_fusion.5
  109.6 0.4 fusion.146
  110.0 0.3 fusion.147
  110.5 0.7 iota_compare_fusion.5
  111.2 0.4 fusion.146
  111.6 0.3 fusion.147
  112.1 0.7 iota_compare_fusion.5
  112.8 0.4 fusion.146
  113.2 0.3 fusion.147
  113.7 0.3 fusion.52
  114.2 0.8 fusion.43
  115.0 3.8 %fusion.46 = (f32[4,128]{1,0:T(4,128)S(1)}, f32[4,128,192]{1,2,0:T(8,128)S(1)}) fusion(bf16[4,128,192]{1,2,0:T(8,128)(2,1)S(1)} %multiply_convert_fusion, bf16[768,192]{1,0:T(8,128)(2,1)S(1)} %all_gather.23, f32[4,128,768]{2,1,0:T(8,128)S(1)} %get-tuple-element.114, u8[128,768]{1,0:T(8,128)(4,1)S(1)} %get-tuple-element.78, ...), kind=kOutput, calls=%fused_computation.80 | convolution fusion | flops 178814464 | bytes 2656256 | tf_op jit(solution)/shard_map/dot_general | solution.py:42
  119.2 14.2 %all_to_all.36 = bf16[128,4,192]{2,1,0:T(4,128)(2,1)S(1)} all-to-all(bf16[128,4,192]{2,1,0:T(4,128)(2,1)S(1)} %copy.33), channel_id=1, replica_groups=mesh['groups'=1,'wide'=8,'narrow'=4] {'wide','narrow'}, dimensions={0} | all-to-all | bytes 393216 | tf_op jit(solution)/shard_map/all_to_all | solution.py:95
  133.6 0.9 copy.35
  (62 shorter events, 3.4 us)
Async XLA Ops:
  0.0 31.8 %copy-start.5 = (s32[4]{0:T(128)S(1)}, s32[4]{0:T(128)}, u32[]{:S(2)}) copy-start(s32[4]{0:T(128)} %param.15) | copy-start | bytes 52
  31.8 9.3 %copy-start = (bf16[4,128,192]{1,2,0:T(8,128)(2,1)S(1)}, bf16[4,128,192]{1,2,0:T(8,128)(2,1)}, u32[]{:S(2)}) copy-start(bf16[4,128,192]{1,2,0:T(8,128)(2,1)} %param.14) | copy-start | bytes 589828
  41.1 6.7 %copy-start.4 = (bf16[48,192]{1,0:T(8,128)(2,1)S(1)}, bf16[48,192]{1,0:T(8,128)(2,1)}, u32[]{:S(2)}) copy-start(bf16[48,192]{1,0:T(8,128)(2,1)} %param.21) | copy-start | bytes 55300
  41.1 23.2 %copy-start.3 = (bf16[48,576]{1,0:T(8,128)(2,1)S(1)}, bf16[48,576]{1,0:T(8,128)(2,1)}, u32[]{:S(2)}) copy-start(bf16[48,576]{1,0:T(8,128)(2,1)} %param.20) | copy-start | bytes 165892
  41.1 36.9 %copy-start.2 = (bf16[48,768]{1,0:T(8,128)(2,1)S(1)}, bf16[48,768]{1,0:T(8,128)(2,1)}, u32[]{:S(2)}) copy-start(bf16[48,768]{1,0:T(8,128)(2,1)} %param.22) | copy-start | bytes 221188
  41.4 50.9 %copy-start.1 = (bf16[192,192]{1,0:T(8,128)(2,1)S(1)}, bf16[192,192]{1,0:T(8,128)(2,1)}, u32[]{:S(2)}) copy-start(bf16[192,192]{1,0:T(8,128)(2,1)} %param.23) | copy-start | bytes 221188
  42.5 64.1 %all-to-all-start = ((bf16[4,128,192]{2,0,1:T(4,128)(2,1)}), bf16[4,128,192]{2,0,1:T(4,128)(2,1)S(1)}, u32[]{:S(2)}, u32[]{:S(2)}) async-start(bf16[4,128,192]{2,0,1:T(4,128)(2,1)} %copy.28), calls=%async_computation | async-start | bytes 524288 | tf_op jit(solution)/shard_map/all_to_all | solution.py:73
where the time goes:
time: 135 us; the launch traced here: 134 us
  blocking collectives  103 us (76%)
  matrix products  13.6 us (10%)
  local copies, waits for them, and re-layouts  6.32 us (5%)
  other arithmetic  5.99 us (4%)
  starting transfers between devices  5.33 us (4%)
    all_gather x1, blocking collectives, body(): lax.all_gather(sample_out, 'narrow', axis=0, tiled=True)  16.4 us
    all_gather x1, blocking collectives, body(): lax.all_gather(feature_out, 'narrow', axis=0, tiled=True)  15.2 us
    all_gather x1, blocking collectives, body(): lax.all_gather(feature_in, 'narrow', axis=0, tiled=True)  14.4 us
    all_gather x1, blocking collectives, body(): lax.all_gather(hidden_up, 'narrow', axis=0, tiled=True)  14.3 us
    all_to_all x1, blocking collectives, body(): lax.all_to_all(result_rows, ('wide', 'narrow'), split_axis=0, concat_axis...  14.2 us
    all_gather x1, blocking collectives, body(): lax.all_gather(hidden_down, 'narrow', axis=0, tiled=True)  14.2 us
    all_gather x1, blocking collectives, body(): lax.all_gather(sample_in, 'narrow', axis=0, tiled=True)  13.8 us
    dot_general x6, matrix products, project(): jnp.dot(flat, weight, preferred_element_type=jnp.float32)  6.72 us
  transfers between devices with their start and end apart: 1, of which 0 were waited for; matrix products, arithmetic and copies ran while one was open for 0% of the time, Pallas kernels for 0%

commit v1 on v0

--- a/solution.py
+++ b/solution.py
@@ -5,6 +5,28 @@
 
 HEADS = 6
 epsilon = 1e-05
+
+
+def in_order(blocks, dim):
+    blocks = jnp.moveaxis(blocks, 0, dim)
+    shape = blocks.shape
+    return blocks.reshape(*shape[:dim], shape[dim] * shape[dim + 1], *shape[dim + 2 :])
+
+
+def doubled(value, axis):
+    count = lax.axis_size(axis)
+    blocks = value[None]
+    for level in range(count.bit_length() - 1):
+        bit = 1 << level
+        other = lax.ppermute(blocks, axis, [(i, i ^ bit) for i in range(count)])
+        both = jnp.stack([blocks, other])
+        upper = lax.axis_index(axis) >> level & 1
+        blocks = jnp.where(upper == 0, both, both[::-1]).reshape(-1, *value.shape)
+    return blocks
+
+
+def doubled_up(value, axis, dim):
+    return in_order(doubled(value, axis), dim)
 
 
 def normalize(values, gain):
@@ -74,7 +96,7 @@
     rows_all, feat_local = (columns.shape[0], columns.shape[1])
     samp_in_all, samp_out_all = (
         lax.all_gather(sample_in, "narrow", axis=0, tiled=True),
-        lax.all_gather(sample_out, "narrow", axis=0, tiled=True),
+        doubled_up(sample_out, "narrow", 0),
     )
     by_feature = jnp.swapaxes(columns, 0, 1)
     valid = jnp.arange(rows_all, dtype=jnp.int32) < train_count[0]

time: 135 us -> 124 us (0.919)
  blocking collectives: 103 us -> 88.5 us
  starting transfers between devices: 5.33 us -> 8.71 us
    all_gather x1 -> x0, blocking collectives: 16.4 us -> none  [body(): lax.all_gather(sample_out, 'narrow', axis=0, tiled=True)]
    all_gather x1, blocking collectives: 14.3 us -> 18.1 us  [body(): lax.all_gather(hidden_up, 'narrow', axis=0, tiled=True)]
    ppermute x0 -> x2, starting transfers between devices: none -> 3.78 us  [doubled(): other = lax.ppermute(blocks, axis, [(i, i ^ bit) for i in range(count)])]
    all_gather x1, blocking collectives: 15.2 us -> 13.7 us  [body(): lax.all_gather(feature_out, 'narrow', axis=0, tiled=True)]
  transfers between devices with their start and end apart: 1 -> 3, of which waited for: 0 -> 0; matrix products, arithmetic and copies ran while one was open for 0% -> 10% of each run, Pallas kernels for 0% -> 0%
where the time goes in v1:
time: 124 us
  blocking collectives  88.5 us (71%)
  matrix products  13.6 us (11%)
  starting transfers between devices  8.71 us (7%)
  local copies, waits for them, and re-layouts  6.32 us (5%)
  other arithmetic  6.07 us (5%)
    all_gather x1, blocking collectives, body(): lax.all_gather(hidden_up, 'narrow', axis=0, tiled=True)  18.1 us
    all_to_all x1, blocking collectives, body(): lax.all_to_all(result_rows, ('wide', 'narrow'), split_axis=0, concat_axis...  14.6 us
    all_gather x1, blocking collectives, body(): lax.all_gather(hidden_down, 'narrow', axis=0, tiled=True)  14.2 us
    all_gather x1, blocking collectives, body(): lax.all_gather(sample_in, 'narrow', axis=0, tiled=True)  14 us
    all_gather x1, blocking collectives, body(): lax.all_gather(feature_in, 'narrow', axis=0, tiled=True)  13.9 us
    all_gather x1, blocking collectives, body(): lax.all_gather(feature_out, 'narrow', axis=0, tiled=True)  13.7 us
    dot_general x6, matrix products, project(): jnp.dot(flat, weight, preferred_element_type=jnp.float32)  6.72 us
    all_to_all x1, starting transfers between devices, body(): lax.all_to_all(first, ('wide', 'narrow'), split_axis=1, concat_axis=0, ti...  4.93 us
  transfers between devices with their start and end apart: 3, of which 0 were waited for; matrix products, arithmetic and copies ran while one was open for 10% of the time, Pallas kernels for 0%

profile of v1, /device:TPU:0, one launch (start us, length us, event | category | flops | bytes accessed | tf_op | source)
XLA Modules:
  0.0 123.9 jit_solution(10382979827139180458)
XLA Ops:
  0.0 3.0 %collective-permute-start = (bf16[1,48,192]{2,1,0:T(8,128)(2,1)}, bf16[1,48,192]{2,1,0:T(8,128)(2,1)S(1)}, u32[]{:S(2)}, u32[]{:S(2)}) collective-permute-start(bf16[1,48,192]{2,1,0:T(8,128)(2,1)} %bitcast.182), channel_id=1, source_target_pairs={{0,1},{1,0},{2,3},{3,2},{4,5},{5,4},{6,7},{7,6},{8,9},{9,8},{10,11... | collective-permute-start | bytes 55304 | tf_op jit(solution)/shard_map/ppermute | solution.py:21
  3.0 0.8 fusion.94
  3.8 13.7 %all_gather.16 = bf16[192,192]{1,0:T(8,128)(2,1)S(1)} all-gather(bf16[48,192]{1,0:T(8,128)(2,1)} %param.19), channel_id=1, replica_groups=mesh['groups'=1,'wide'=8,'narrow'=4] {'narrow'}, dimensions={0}, use_global_device_ids=true | all-gather | bytes 92160 | tf_op jit(solution)/shard_map/all_gather | solution.py:84
  17.5 13.9 %all_gather.15 = bf16[192,576]{1,0:T(8,128)(2,1)S(1)} all-gather(bf16[48,576]{1,0:T(8,128)(2,1)} %param.18), channel_id=1, replica_groups=mesh['groups'=1,'wide'=8,'narrow'=4] {'narrow'}, dimensions={0}, use_global_device_ids=true | all-gather | bytes 276480 | tf_op jit(solution)/shard_map/all_gather | solution.py:83
  31.4 1.3 %convolution_convert_fusion.3 = bf16[4,128,576]{1,2,0:T(8,128)(2,1)S(1)} fusion(bf16[4,128,192]{1,2,0:T(8,128)(2,1)} %param.14, bf16[192,576]{1,0:T(8,128)(2,1)S(1)} %all_gather.15), kind=kOutput, calls=%fused_computation.55 | convolution fusion | flops 113541120 | bytes 1007616 | tf_op jit(solution)/shard_map/dot_general | solution.py:64
  32.8 9.3 %while.22 = (s32[]{:T(128)}, bf16[4,128,192]{1,2,0:T(8,128)(2,1)S(1)}, bf16[4,128,576]{1,2,0:T(8,128)(2,1)S(1)}, s32[4]{0:T(128)S(1)}, s32[]{:T(128)}) while((s32[]{:T(128)}, bf16[4,128,192]{1,2,0:T(8,128)(2,1)S(1)}, bf16[4,128,576]{1,2,0:T(8,128)(2,1)S(1)}, s32[4]{0:T(128)S(1)}, s32[]{:T(128)}) %tuple.62), condition=%wide.region_3.4_spmd.clone, body=%wide.region_0.3_spmd.clone.sunk | while | flops 19981440 | bytes 1776221 | solution.py:92
  32.8 0.7 dynamic_slice.20
  33.5 0.7 iota_compare_fusion.4
  34.2 0.4 fusion.138
  34.6 0.3 fusion.139
  35.1 0.7 dynamic_slice.20
  35.8 0.7 iota_compare_fusion.4
  36.5 0.4 fusion.138
  36.9 0.3 fusion.139
  37.4 0.7 dynamic_slice.20
  38.1 0.7 iota_compare_fusion.4
  38.9 0.4 fusion.138
  39.2 0.3 fusion.139
  39.8 0.7 dynamic_slice.20
  40.4 0.7 iota_compare_fusion.4
  41.2 0.4 fusion.138
  41.5 0.3 fusion.139
  42.1 0.3 fusion.95
  42.6 0.9 copy.30
  43.5 4.9 %all-to-all-start = ((bf16[4,128,192]{2,0,1:T(4,128)(2,1)}), bf16[4,128,192]{2,0,1:T(4,128)(2,1)S(1)}, u32[]{:S(2)}, u32[]{:S(2)}) async-start(bf16[4,128,192]{2,0,1:T(4,128)(2,1)} %copy.30), calls=%async_computation | async-start | bytes 524288 | tf_op jit(solution)/shard_map/all_to_all | solution.py:95
  48.4 18.1 %all_gather.18 = bf16[192,768]{1,0:T(8,128)(2,1)S(1)} all-gather(bf16[48,768]{1,0:T(8,128)(2,1)S(1)} %copy-done.2), channel_id=1, replica_groups=mesh['groups'=1,'wide'=8,'narrow'=4] {'narrow'}, dimensions={0}, use_global_device_ids=true | all-gather | bytes 368640 | tf_op jit(solution)/shard_map/all_gather | solution.py:110
  66.5 14.2 %all_gather.19 = bf16[768,192]{1,0:T(8,128)(2,1)S(1)} all-gather(bf16[192,192]{1,0:T(8,128)(2,1)S(1)} %copy-done.1), channel_id=1, replica_groups=mesh['groups'=1,'wide'=8,'narrow'=4] {'narrow'}, dimensions={0}, use_global_device_ids=true | all-gather | bytes 368640 | tf_op jit(solution)/shard_map/all_gather | solution.py:111
  80.7 0.8 collective-permute-start.1
  81.5 14.0 %all_gather.17 = bf16[192,576]{1,0:T(8,128)(2,1)S(1)} all-gather(bf16[48,576]{1,0:T(8,128)(2,1)S(1)} %copy-done.3), channel_id=1, replica_groups=mesh['groups'=1,'wide'=8,'narrow'=4] {'narrow'}, dimensions={0}, use_global_device_ids=true | all-gather | bytes 276480 | tf_op jit(solution)/shard_map/all_gather | solution.py:98
  96.0 0.4 convolution_convert_fusion.2
  96.4 6.4 %while.23 = (s32[]{:T(128)}, bf16[4,128,192]{1,2,0:T(8,128)(2,1)S(1)}, bf16[4,128,576]{1,2,0:T(8,128)(2,1)S(1)}, s32[]{:T(128)}, s32[]{:T(128)}) while((s32[]{:T(128)}, bf16[4,128,192]{1,2,0:T(8,128)(2,1)S(1)}, bf16[4,128,576]{1,2,0:T(8,128)(2,1)S(1)}, s32[]{:T(128)}, s32[]{:T(128)}) %tuple.59), condition=%wide.region_9.10_spmd.clone, body=%wide.region_6.9_spmd.clone.sunk | while | flops 19981440 | bytes 1776209 | solution.py:104
  96.4 0.7 iota_compare_fusion.5
  97.1 0.4 fusion.147
  97.4 0.3 fusion.148
  98.0 0.7 iota_compare_fusion.5
  98.7 0.4 fusion.147
  99.0 0.3 fusion.148
  99.6 0.7 iota_compare_fusion.5
  100.3 0.4 fusion.147
  100.7 0.3 fusion.148
  101.2 0.7 iota_compare_fusion.5
  101.9 0.4 fusion.147
  102.3 0.3 fusion.148
  102.8 0.3 fusion.52
  103.3 0.8 fusion.43
  104.1 3.8 %fusion.46 = (f32[4,128]{1,0:T(4,128)S(1)}, f32[4,128,192]{1,2,0:T(8,128)S(1)}) fusion(bf16[4,128,192]{1,2,0:T(8,128)(2,1)S(1)} %multiply_convert_fusion, bf16[768,192]{1,0:T(8,128)(2,1)S(1)} %all_gather.19, f32[4,128,768]{2,1,0:T(8,128)S(1)} %get-tuple-element.116, u8[128,768]{1,0:T(8,128)(4,1)S(1)} %get-tuple-element.78, ...), kind=kOutput, calls=%fused_computation.80 | convolution fusion | flops 178814464 | bytes 2656256 | tf_op jit(solution)/shard_map/dot_general | solution.py:64
  108.3 14.6 %all_to_all.36 = bf16[128,4,192]{2,1,0:T(4,128)(2,1)S(1)} all-to-all(bf16[128,4,192]{2,1,0:T(4,128)(2,1)S(1)} %copy.36), channel_id=1, replica_groups=mesh['groups'=1,'wide'=8,'narrow'=4] {'wide','narrow'}, dimensions={0} | all-to-all | bytes 393216 | tf_op jit(solution)/shard_map/all_to_all | solution.py:117
  123.0 0.9 copy.38
  (69 shorter events, 3.7 us)
Async XLA Ops:
  0.0 32.8 %copy-start.5 = (s32[4]{0:T(128)S(1)}, s32[4]{0:T(128)}, u32[]{:S(2)}) copy-start(s32[4]{0:T(128)} %param.15) | copy-start | bytes 52
  0.0 80.7 %collective-permute-start = (bf16[1,48,192]{2,1,0:T(8,128)(2,1)}, bf16[1,48,192]{2,1,0:T(8,128)(2,1)S(1)}, u32[]{:S(2)}, u32[]{:S(2)}) collective-permute-start(bf16[1,48,192]{2,1,0:T(8,128)(2,1)} %bitcast.182), channel_id=1, source_target_pairs={{0,1},{1,0},{2,3},{3,2},{4,5},{5,4},{6,7},{7,6},{8,9},{9,8},{10,11... | collective-permute-start | bytes 55304 | tf_op jit(solution)/shard_map/ppermute | solution.py:21
  32.8 9.3 %copy-start = (bf16[4,128,192]{1,2,0:T(8,128)(2,1)S(1)}, bf16[4,128,192]{1,2,0:T(8,128)(2,1)}, u32[]{:S(2)}) copy-start(bf16[4,128,192]{1,2,0:T(8,128)(2,1)} %param.14) | copy-start | bytes 589828
  42.1 6.3 %copy-start.2 = (bf16[48,768]{1,0:T(8,128)(2,1)S(1)}, bf16[48,768]{1,0:T(8,128)(2,1)}, u32[]{:S(2)}) copy-start(bf16[48,768]{1,0:T(8,128)(2,1)} %param.22) | copy-start | bytes 221188
  42.1 24.4 %copy-start.1 = (bf16[192,192]{1,0:T(8,128)(2,1)S(1)}, bf16[192,192]{1,0:T(8,128)(2,1)}, u32[]{:S(2)}) copy-start(bf16[192,192]{1,0:T(8,128)(2,1)} %param.23) | copy-start | bytes 221188
  42.4 38.3 %copy-start.4 = (bf16[48,192]{1,0:T(8,128)(2,1)S(1)}, bf16[48,192]{1,0:T(8,128)(2,1)}, u32[]{:S(2)}) copy-start(bf16[48,192]{1,0:T(8,128)(2,1)} %param.21) | copy-start | bytes 55300
  42.4 39.1 %copy-start.3 = (bf16[48,576]{1,0:T(8,128)(2,1)S(1)}, bf16[48,576]{1,0:T(8,128)(2,1)}, u32[]{:S(2)}) copy-start(bf16[48,576]{1,0:T(8,128)(2,1)} %param.20) | copy-start | bytes 165892
  43.5 52.1 %all-to-all-start = ((bf16[4,128,192]{2,0,1:T(4,128)(2,1)}), bf16[4,128,192]{2,0,1:T(4,128)(2,1)S(1)}, u32[]{:S(2)}, u32[]{:S(2)}) async-start(bf16[4,128,192]{2,0,1:T(4,128)(2,1)} %copy.30), calls=%async_computation | async-start | bytes 524288 | tf_op jit(solution)/shard_map/all_to_all | solution.py:95
  80.7 14.8 %collective-permute-start.1 = (bf16[2,48,192]{2,1,0:T(8,128)(2,1)S(1)}, bf16[2,48,192]{2,1,0:T(8,128)(2,1)S(1)}, u32[]{:S(2)}, u32[]{:S(2)}) collective-permute-start(bf16[2,48,192]{2,1,0:T(8,128)(2,1)S(1)} %get-tuple-element.102), channel_id=1, source_target_pairs={{0,2},{1,3},{2,0},{3,1},{4,6},{5,7},{6,4},{7,5},{8,10},{9,11},{10,... | collective-permute-start | bytes 110600 | tf_op jit(solution)/shard_map/ppermute | solution.py:21
